TPU v7x, 256 devices: a whole 4x4x8 slice. The times are simulated.
256 devices in a mesh: grp: 8 (over z), tp: 32 (over x, y, core).
Axes of the slice: x: 4, y: 4, z: 8, core: 2. Of those that a mesh axis runs over, the one named last changes fastest.
Arguments:
- hidden_in: bfloat16 [1024, 3584], P(('grp', 'tp')), may hold values from -6 to 6
- norm_gains: float32 [4, 3584], replicated, may hold values from 0.25 to 1.75
- w_qkv: bfloat16 [3584, 8192], P(None, 'tp'), may hold values from -0.09375 to 0.09375
- w_out: bfloat16 [4096, 3584], P('tp'), may hold values from -0.09375 to 0.09375
- w_gate_up: bfloat16 [2, 3584, 8192], P(None, None, 'tp'), may hold values from -0.09375 to 0.09375
- w_down: bfloat16 [8192, 3584], P('tp'), may hold values from -0.0625 to 0.0625
- prompt_keys: bfloat16 [32768, 2048], P(('grp', 'tp')), may hold values from -480 to 480, as said below
- prompt_values: bfloat16 [32768, 2048], P(('grp', 'tp')), may hold values from -6 to 6
- tail_keys: bfloat16 [1024, 64, 2048], P(('grp', 'tp')), may hold values from -480 to 480, as said below
- tail_values: bfloat16 [1024, 64, 2048], P(('grp', 'tp')), may hold values from -6 to 6
- prompt_len: int32 [80], replicated, may hold values from 1 to 4087, as said below
- group_home: int32 [80], replicated, may hold values from 0 to 7, as said below
- req_group: int32 [1024], P('grp'), may hold values from 0 to 79, as said below
- tail_len: int32 [1024], P('grp'), may hold values from 1 to 64, 32768 in all
Outputs:
- layer_out: bfloat16 [1024, 3584], P(('grp', 'tp'))
Inputs may be any that keep to these rules, and one draw needn't show every extreme that they name: `group_home`: each grp device is home to exactly 10 groups. `prompt_len`: the prompts of the groups homed on one grp device lie one after another in order of group id from the first of that device's 4096 cache positions; together they hold at most 4096 positions, exactly 4096 on one home in every draw, where one group holds 4087 of them. `req_group`: of the 128 requests held by one grp device, at most 32 belong to groups homed on any one grp device; in every draw one home receives exactly 32 requests from every grp device. `prompt_keys`: cached keys, already rotated. `tail_keys`: cached keys, already rotated.
All inputs are finite; a program needn't handle non-finite values. No bound on the sum of `tail_len` on one device may be relied on, other than what follows from the above.
Results may differ from a plain program's by a relative error of at most 0.015.
Values may be sent and summed in bfloat16 or wider, within the bound.
A program may use at most 128 MiB of HBM per device.

v0:
```python
import math
import jax
import jax.numpy as jnp
from jax import lax
from jax.sharding import PartitionSpec as P

HEADS = 16
KV_HEADS = 8
HEAD_DIM = 256
NORM_EPS = 1e-06
SOFT_CAP = 50.0


def rms_scale(values, gain_row):
    values = values.astype(jnp.float32)
    return (
        values * lax.rsqrt(jnp.mean(values * values, axis=-1, keepdims=True) + NORM_EPS) * gain_row
    )


def rotate(head_rows, position):
    half_width = head_rows.shape[-1] // 2
    freq_index = jnp.arange(half_width).astype(jnp.float32)
    frequency = jnp.exp(freq_index * (-math.log(10000.0) / half_width))
    angles = position.astype(jnp.float32)[:, None] * frequency[None, :]
    cosine = jnp.cos(angles)[:, None, :]
    sine_part = jnp.sin(angles)[:, None, :]
    head_rows = head_rows.astype(jnp.float32)
    first_half = head_rows[..., :half_width]
    second = head_rows[..., half_width:]
    return jnp.concatenate(
        [first_half * cosine - second * sine_part, second * cosine + first_half * sine_part],
        axis=-1,
    )


def capped(scores):
    return SOFT_CAP * jnp.tanh(scores * HEAD_DIM ** (-0.5) / SOFT_CAP)


def lookup(lookup_table, index_list):
    matches = index_list[:, None] == jnp.arange(lookup_table.shape[0], dtype=jnp.int32)[None, :]
    return jnp.sum(jnp.where(matches, lookup_table[None, :], 0), axis=1)


def group_starts(prompt_len, group_home):
    group_ids = jnp.arange(prompt_len.shape[0], dtype=jnp.int32)
    same_home = group_home[:, None] == group_home[None, :]
    earlier = group_ids[None, :] < group_ids[:, None]
    return jnp.sum(jnp.where(same_home & earlier, prompt_len[None, :], 0), axis=1)


def shared_part(queries, key_rows, value_rows, visible):
    scores = capped(
        jnp.einsum("nkjd,pkd->nkjp", queries, key_rows, preferred_element_type=jnp.float32)
    )
    exponent = jnp.where(visible[:, None, None, :], jnp.exp(scores), 0.0)
    numerator = jnp.einsum(
        "nkjp,pkd->nkjd",
        exponent.astype(jnp.bfloat16),
        value_rows,
        preferred_element_type=jnp.float32,
    )
    return (numerator, jnp.sum(exponent, axis=-1))


def own_part(queries, key_rows, value_rows, visible):
    scores = capped(
        jnp.einsum("nkjd,npkd->nkjp", queries, key_rows, preferred_element_type=jnp.float32)
    )
    exponent = jnp.where(visible[:, None, None, :], jnp.exp(scores), 0.0)
    numerator = jnp.einsum(
        "nkjp,npkd->nkjd",
        exponent.astype(jnp.bfloat16),
        value_rows,
        preferred_element_type=jnp.float32,
    )
    return (numerator, jnp.sum(exponent, axis=-1))


def per_device(
    hidden_in,
    norm_gains,
    w_qkv,
    w_out,
    w_gate_up,
    w_down,
    prompt_keys,
    prompt_values,
    tail_keys,
    tail_values,
    prompt_len,
    group_home,
    req_group,
    tail_len,
):
    tp_rank = lax.axis_index("tp")
    q_width = HEADS * HEAD_DIM
    kv_width = KV_HEADS * HEAD_DIM
    row_count = hidden_in.shape[0]
    normed = rms_scale(hidden_in, norm_gains[0]).astype(jnp.bfloat16)
    qkv_share = jnp.dot(
        lax.all_gather(normed, "tp", axis=0, tiled=True), w_qkv, preferred_element_type=jnp.float32
    ).astype(jnp.bfloat16)
    projected_qkv = lax.all_gather(qkv_share, "tp", axis=1, tiled=True)
    requests = projected_qkv.shape[0]
    req_len = lookup(prompt_len, req_group)
    position = req_len + tail_len
    queries = rotate(
        projected_qkv[:, :q_width].reshape(requests, HEADS, HEAD_DIM), position
    ).astype(jnp.bfloat16)
    queries = queries.reshape(requests, KV_HEADS, 2, HEAD_DIM)
    key_new = rotate(
        projected_qkv[:, q_width : q_width + kv_width].reshape(requests, KV_HEADS, HEAD_DIM),
        position,
    ).astype(jnp.bfloat16)
    value_new = projected_qkv[:, q_width + kv_width :].reshape(requests, KV_HEADS, HEAD_DIM)
    starts = group_starts(prompt_len, group_home)
    req_home = lookup(group_home, req_group)
    req_start = lookup(starts, req_group)
    cap_dev = prompt_keys.shape[0]
    row_first = tp_rank * row_count
    own_queries = lax.dynamic_slice_in_dim(queries, row_first, row_count, 0)
    own_tail_len = lax.dynamic_slice_in_dim(tail_len, row_first, row_count, 0)
    tail_dev = tail_keys.shape[1]
    tail_pos = jnp.arange(tail_dev, dtype=jnp.int32)
    own_num, own_den = own_part(
        own_queries,
        tail_keys.reshape(row_count, tail_dev, KV_HEADS, HEAD_DIM),
        tail_values.reshape(row_count, tail_dev, KV_HEADS, HEAD_DIM),
        tail_pos[None, :] < own_tail_len[:, None],
    )
    numerator = lax.dynamic_update_slice_in_dim(
        jnp.zeros((requests, KV_HEADS, 2, HEAD_DIM), jnp.float32), own_num, row_first, 0
    )
    denominator = lax.dynamic_update_slice_in_dim(
        jnp.zeros((requests, KV_HEADS, 2), jnp.float32), own_den, row_first, 0
    )
    key_piece = lax.all_gather(prompt_keys, "grp", axis=0, tiled=True)
    value_piece = lax.all_gather(prompt_values, "grp", axis=0, tiled=True)
    piece_rows = key_piece.shape[0]
    gathered_index = jnp.arange(piece_rows, dtype=jnp.int32)
    home_index = gathered_index // cap_dev
    piece_offsets = tp_rank * cap_dev + gathered_index % cap_dev
    visible = (
        (home_index[None, :] == req_home[:, None])
        & (piece_offsets[None, :] >= req_start[:, None])
        & (piece_offsets[None, :] < (req_start + req_len)[:, None])
    )
    part_num, part_den = shared_part(
        queries,
        key_piece.reshape(piece_rows, KV_HEADS, HEAD_DIM),
        value_piece.reshape(piece_rows, KV_HEADS, HEAD_DIM),
        visible,
    )
    numerator, denominator = (numerator + part_num, denominator + part_den)
    share_width = w_out.shape[0]
    first_col = tp_rank * share_width
    flat_num = numerator.reshape(requests, q_width)
    flat_den = denominator.reshape(requests, HEADS)
    total_num, total_den = lax.psum((flat_num, flat_den), "tp")
    share_num = lax.dynamic_slice_in_dim(total_num, first_col, share_width, 1)
    self_exp = jnp.exp(
        capped(jnp.einsum("nkjd,nkd->nkj", queries, key_new, preferred_element_type=jnp.float32))
    )
    self_num = (
        lax.optimization_barrier(self_exp.astype(jnp.bfloat16)).astype(jnp.float32)[..., None]
        * value_new.astype(jnp.float32)[:, :, None, :]
    )
    self_share = lax.dynamic_slice_in_dim(
        self_num.reshape(requests, q_width), first_col, share_width, 1
    )
    total_den = total_den + self_exp.reshape(requests, HEADS)
    head_of_col = (first_col + jnp.arange(share_width, dtype=jnp.int32)) // HEAD_DIM
    head_pick = (head_of_col[None, :] == jnp.arange(HEADS, dtype=jnp.int32)[:, None]).astype(
        jnp.float32
    )
    den_cols = jnp.dot(total_den, head_pick, precision=lax.Precision.HIGHEST)
    attn_share = ((share_num + self_share) / den_cols).astype(jnp.bfloat16)
    block_rows = attn_share
    attn_proj = lax.psum_scatter(
        jnp.dot(block_rows, w_out, preferred_element_type=jnp.float32),
        "tp",
        scatter_dimension=0,
        tiled=True,
    )
    resid = (hidden_in.astype(jnp.float32) + rms_scale(attn_proj, norm_gains[1])).astype(
        jnp.bfloat16
    )
    ffn_in = rms_scale(resid, norm_gains[2]).astype(jnp.bfloat16)
    gate_up = jnp.einsum(
        "rd,kdf->krf",
        lax.all_gather(ffn_in, "tp", axis=0, tiled=True),
        w_gate_up,
        preferred_element_type=jnp.float32,
    )
    hidden_units = (jax.nn.gelu(gate_up[0], approximate=True) * gate_up[1]).astype(jnp.bfloat16)
    block_rows = hidden_units
    ffn_proj = lax.psum_scatter(
        jnp.dot(block_rows, w_down, preferred_element_type=jnp.float32).astype(jnp.bfloat16),
        "tp",
        scatter_dimension=0,
        tiled=True,
    ).astype(jnp.float32)
    return (resid.astype(jnp.float32) + rms_scale(ffn_proj, norm_gains[3])).astype(jnp.bfloat16)


def solution(mesh):
    in_specs = (
        P(("grp", "tp"), None),
        P(),
        P(None, "tp"),
        P("tp", None),
        P(None, None, "tp"),
        P("tp", None),
        P(("grp", "tp"), None),
        P(("grp", "tp"), None),
        P(("grp", "tp"), None, None),
        P(("grp", "tp"), None, None),
        P(),
        P(),
        P("grp"),
        P("grp"),
    )
    out_specs = P(("grp", "tp"), None)
    return jax.shard_map(
        per_device, mesh=mesh, in_specs=in_specs, out_specs=out_specs, check_vma=False
    )
```

profile of v0, /device:TPU:1, one launch (start us, length us, event | category | flops | bytes accessed | tf_op | source)
XLA Modules:
  0.0 625.6 jit_solution(4266515688802575155)
XLA Ops:
  6.5 1.2 slice_reduce_fusion.1
  7.7 0.9 fusion.35
  8.6 0.8 fusion.47
  9.5 26.6 %all-gather = bf16[32,4,3584]{2,1,0:T(4,128)(2,1)S(1)} all-gather(bf16[1,4,3584]{2,1,0:T(4,128)(2,1)S(1)} %fusion.47), channel_id=1, replica_groups=mesh['grp'=8,'tp'=32] {'tp'}, dimensions={0}, use_global_device_ids=true | all-gather | bytes 946176 | tf_op jit(solution)/shard_map/all_gather | solution.py:103
  36.0 1.1 reshape.279
  37.2 2.9 convolution_convert_fusion.1
  40.1 1.0 copy.77
  41.2 1.0 copy.79
  42.3 0.0 all-reduce.6.cloned.1.call-start
  42.3 0.1 dynamic_slice.12
  42.5 0.2 select_reduce_fusion.2
  42.6 0.1 select_reduce_fusion.3
  42.8 0.1 iota_compare_fusion.4
  42.8 0.3 multiply_cosine_fusion
  43.1 0.9 compare_and_fusion
  44.0 46.5 %all-gather.6.cloned.1.call-done = bf16[128,8192]{1,0:T(8,128)(2,1)} async-done(((bf16[128,256]{1,0:T(8,128)(2,1)}), bf16[128,8192]{1,0:T(8,128)(2,1)}) %all-gather.6.cloned.1.call-update) | async-done | bytes 2097168 | tf_op jit(solution)/shard_map/all_gather | solution.py:105
  90.5 1.4 slice_convert_fusion
  91.9 0.7 copy.101
  92.6 0.3 subtract_convert_fusion
  92.9 0.1 copy.75
  93.1 0.1 copy.76
  93.2 0.9 copy-done.11
  94.1 0.5 fusion.73
  94.6 0.1 copy.88
  94.7 2.4 slice_convert_fusion.2
  97.2 0.3 copy.102
  97.5 0.1 subtract_convert_fusion.1
  97.7 0.1 maximum_bitcast_fusion
  97.8 1.2 pad_maximum_fusion
  98.9 0.3 fusion.10
  99.2 50.9 %all-gather.8.cloned.1.call-done = bf16[1024,2048]{0,1:T(8,128)(2,1)} async-done(((bf16[128,2048]{0,1:T(8,128)(2,1)}), bf16[1024,2048]{0,1:T(8,128)(2,1)}) %all-gather.8.cloned.1.call-update) | async-done | bytes 4194320 | tf_op jit(solution)/shard_map/all_gather | solution.py:139
  150.1 7.7 %bitcast_reduce_fusion = (f32[128,8,2]{0,2,1:T(2,128)S(1)}, f32[8,128,2,1024]{3,1,2,0:T(8,128)}) fusion(pred[128,1024]{1,0:T(8,128)(4,1)} %compare_and_fusion, bf16[1024,8,256,1]{0,2,3,1:T(8,128)(2,1)} %bitcast.96, bf16[128,8,2,128]{3,0,2,1:T(8,128)(2,1)S(1)} %bitcast.87, bf16[128,8,2,128]{3,0,2,1:T(8,128)(2,1)S(1)} %bitcast.84), kind=kOutput, calls=%fused_computation | convolution fusion | flops 1084225536 | bytes 13770752 | tf_op jit(solution)/shard_map/nkjd,pkd->nkjp/dot_general | solution.py:55
  157.8 55.1 %all-gather.10.cloned.1.call-done = bf16[1024,2048]{0,1:T(8,128)(2,1)} async-done(((bf16[128,2048]{0,1:T(8,128)(2,1)}), bf16[1024,2048]{0,1:T(8,128)(2,1)}) %all-gather.10.cloned.1.call-update) | async-done | bytes 4194320 | tf_op jit(solution)/shard_map/all_gather | solution.py:140
  212.9 7.0 %fusion = f32[8,128,2,256]{3,1,2,0:T(8,128)S(1)} fusion(bf16[1024,8,256,1]{0,2,3,1:T(8,128)(2,1)} %bitcast.97, f32[8,128,2,1024]{3,1,2,0:T(8,128)} %get-tuple-element.27, pred[128,1024]{1,0:T(8,128)(4,1)} %compare_and_fusion), kind=kOutput, calls=%fused_computation.4 | convolution fusion | flops 1082130432 | bytes 14811136 | tf_op jit(solution)/shard_map/nkjp,pkd->nkjd/dot_general | solution.py:58
  220.0 1.4 copy.123
  221.3 0.7 fusion.28
  222.0 2.9 copy.85
  224.9 2.9 copy.86
  227.8 0.2 all-reduce.8.cloned.1.call-start
  228.1 3.4 fusion.15
  231.4 1.2 copy.94
  232.7 0.2 copy.87
  232.9 0.3 copy.103
  233.3 2.8 broadcast_multiply_fusion
  236.1 4.0 mul.269
  240.1 0.1 dynamic-slice_add_fusion
  240.2 1.3 add.147
  241.4 67.5 %psum.15 = f32[128,16]{0,1:T(8,128)S(1)} all-reduce(f32[128,16]{0,1:T(8,128)S(1)} %bitcast.94), channel_id=1, replica_groups=mesh['grp'=8,'tp'=32] {'tp'}, use_global_device_ids=true, to_apply=%region_8.9 | all-reduce | flops 2048 | bytes 16384 | tf_op jit(solution)/shard_map/psum | solution.py:161
  309.0 38.9 %all-reduce.6.cloned.1.call-done = f32[128,4096]{1,0:T(8,128)} async-done(((f32[128,4096]{1,0:T(8,128)}), f32[128,4096]{1,0:T(8,128)}) %all-reduce.6.cloned.1.call-update) | async-done | bytes 2097168 | tf_op jit(solution)/shard_map/psum | solution.py:161
  347.9 1.1 fusion.5
  349.1 1.6 fusion.74
  350.7 0.0 all-reduce.10.cloned.1.call-start
  350.8 0.6 dynamic-slice.6
  352.0 115.3 %all-reduce.8.cloned.1.call-done = f32[128,3584]{1,0:T(8,128)} async-done(((f32[128,3584]{1,0:T(8,128)}), f32[128,3584]{1,0:T(8,128)}) %all-reduce.8.cloned.1.call-update) | async-done | bytes 1835024
  467.4 1.0 multiply_reduce_fusion
  468.4 1.1 fusion.39
  469.5 0.1 fusion.46
  469.6 28.2 %all-gather.1 = bf16[32,4,3584]{2,1,0:T(4,128)(2,1)} all-gather(bf16[1,4,3584]{2,1,0:T(4,128)(2,1)S(1)} %fusion.46), channel_id=1, replica_groups=mesh['grp'=8,'tp'=32] {'tp'}, dimensions={0}, use_global_device_ids=true | all-gather | bytes 946176 | tf_op jit(solution)/shard_map/all_gather | solution.py:193
  497.9 1.7 reshape.286
  499.5 2.7 convolution_bitcast_fusion
  502.2 1.4 convolution_convert_fusion
  503.7 112.7 %all-reduce.10.cloned.1.call-done = bf16[128,3584]{1,0:T(8,128)(2,1)} async-done(((bf16[128,3584]{1,0:T(8,128)(2,1)}), bf16[128,3584]{1,0:T(8,128)(2,1)}) %all-reduce.10.cloned.1.call-update) | async-done | bytes 917520
  616.3 1.0 fusion.33
  617.3 1.5 fusion.42
  (45 shorter events, 0.4 us)
Async XLA Ops:
  6.5 495.7 %copy-start = (bf16[256,3584]{1,0:T(8,128)(2,1)S(1)}, bf16[256,3584]{1,0:T(8,128)(2,1)}, u32[]{:S(2)}) copy-start(bf16[256,3584]{1,0:T(8,128)(2,1)} %param.19) | copy-start | bytes 5505028
  6.5 83.9 %all-gather.6.cloned.1.call-start = ((), (), s32[]{:S(2)}) async-start(), calls=%async_computation | async-start | bytes 2162688 | tf_op jit(solution)/shard_map/all_gather | solution.py:105
  36.0 4.1 copy-start.4
  37.2 4.0 copy-start.5
  40.0 2.3 copy-start.10
  40.1 2.4 copy-start.7
  40.1 2.4 copy-start.8
  40.1 2.6 copy-start.9
  40.1 110.0 %all-gather.8.cloned.1.call-start = ((), (), s32[]{:S(2)}) async-start(), calls=%async_computation.1 | async-start | bytes 4718592 | tf_op jit(solution)/shard_map/all_gather | solution.py:139
  41.2 171.8 %all-gather.10.cloned.1.call-start = ((), (), s32[]{:S(2)}) async-start(), calls=%async_computation.2 | async-start | bytes 4718592 | tf_op jit(solution)/shard_map/all_gather | solution.py:140
  42.3 305.7 %all-reduce.6.cloned.1.call-start = ((), (), s32[]{:S(2)}) async-start(), calls=%async_computation.3 | async-start | bytes 4194304 | tf_op jit(solution)/shard_map/psum | solution.py:161
  92.9 1.2 copy-start.11
  97.5 1.4 copy-start.2
  227.8 5.1 copy-start.1
  227.8 239.5 %all-reduce.8.cloned.1.call-start = ((), (), s32[]{:S(2)}) async-start(), calls=%async_computation.4 | async-start | bytes 3670016
  236.1 113.0 %copy-start.3 = (bf16[128,3584]{1,0:T(8,128)(2,1)S(1)}, bf16[128,3584]{1,0:T(8,128)(2,1)}, u32[]{:S(2)}) copy-start(bf16[128,3584]{1,0:T(8,128)(2,1)} %param.17) | copy-start | bytes 2752516
  349.1 1.7 copy-start.12
  349.1 119.3 %copy-start.6 = (bf16[4,3584]{1,0:T(4,128)(2,1)S(1)}, bf16[4,3584]{1,0:T(4,128)(2,1)}, u32[]{:S(2)}) copy-start(bf16[4,3584]{1,0:T(4,128)(2,1)} %param.14) | copy-start | bytes 86020
  350.7 265.6 %all-reduce.10.cloned.1.call-start = ((), (), s32[]{:S(2)}) async-start(), calls=%async_computation.5 | async-start | bytes 1835008
Sparse Core Ops, SparseCore 0:
  40.2 50.2 all-gather.5
  92.2 57.8 all-gather.7
  151.8 61.1 all-gather.9
  228.0 119.9 all-reduce.5
  351.1 116.2 all-reduce.7
  503.8 112.4 all-reduce.9
where the time goes:
time: 626 us
  waiting for transfers between devices  419 us (67%)
  blocking collectives  122 us (19%)
  matrix products  28.5 us (5%)
  local copies, waits for them, and re-layouts  23.3 us (4%)
  other arithmetic  17.2 us (3%)
  between operations  14.4 us (2%)
    unnamed x8, waiting for transfers between devices  228 us
    psum x1, blocking collectives, per_device(): total_num, total_den = lax.psum((flat_num, flat_den), 'tp')  67.5 us
    all_gather x1, waiting for transfers between devices, per_device(): value_piece = lax.all_gather(prompt_values, 'grp', axis=0, tiled=True)  55.1 us
    all_gather x1, waiting for transfers between devices, per_device(): key_piece = lax.all_gather(prompt_keys, 'grp', axis=0, tiled=True)  50.9 us
    all_gather x1, waiting for transfers between devices, per_device(): projected_qkv = lax.all_gather(qkv_share, 'tp', axis=1, tiled=True)  46.5 us
    psum x1, waiting for transfers between devices, per_device(): total_num, total_den = lax.psum((flat_num, flat_den), 'tp')  38.9 us
    all_gather x1, blocking collectives, per_device(): lax.all_gather(ffn_in, 'tp', axis=0, tiled=True)  28.2 us
    all_gather x1, blocking collectives, per_device(): lax.all_gather(normed, 'tp', axis=0, tiled=True)  26.6 us
  transfers between devices with their start and end apart: 6, of which 6 were waited for; matrix products, arithmetic and copies ran while one was open for 5% of the time, Pallas kernels for 0%

commit v1 on v0

--- a/solution.py
+++ b/solution.py
@@ -137,7 +137,9 @@
         jnp.zeros((requests, KV_HEADS, 2), jnp.float32), own_den, row_first, 0
     )
     key_piece = lax.all_gather(prompt_keys, "grp", axis=0, tiled=True)
-    value_piece = lax.all_gather(prompt_values, "grp", axis=0, tiled=True)
+    value_piece = jnp.concatenate(
+        lax.all_to_all(jnp.stack([prompt_values] * lax.axis_size("grp")), "grp", 0, 0), axis=0
+    )
     piece_rows = key_piece.shape[0]
     gathered_index = jnp.arange(piece_rows, dtype=jnp.int32)
     home_index = gathered_index // cap_dev

time: 626 us -> 599 us (0.957)
  waiting for transfers between devices: 419 us -> 385 us
  local copies, waits for them, and re-layouts: 23.3 us -> 32.7 us
  starting transfers between devices: 0.39 us -> 8.89 us
  matrix products: 28.5 us -> 21.3 us
    all_to_all x0 -> x1, waiting for transfers between devices: none -> 60.4 us  [per_device(): lax.all_to_all(jnp.stack([prompt_values] * lax.axis_size('grp')), 'grp',...]
    all_gather x1 -> x0, waiting for transfers between devices: 55.1 us -> none  [per_device(): value_piece = lax.all_gather(prompt_values, 'grp', axis=0, tiled=True)]
    all_gather x1, waiting for transfers between devices: 50.9 us -> 21.5 us  [per_device(): key_piece = lax.all_gather(prompt_keys, 'grp', axis=0, tiled=True)]
    all_gather x1, waiting for transfers between devices: 46.5 us -> 36.5 us  [per_device(): projected_qkv = lax.all_gather(qkv_share, 'tp', axis=1, tiled=True)]
    all_to_all x0 -> x1, starting transfers between devices: none -> 8.33 us  [per_device(): lax.all_to_all(jnp.stack([prompt_values] * lax.axis_size('grp')), 'grp',...]
    unnamed x35 -> x41, local copies, waits for them, and re-layouts: 9.03 us -> 16 us
    unnamed x8 -> x7, waiting for transfers between devices: 228 us -> 228 us
  transfers between devices with their start and end apart: 6 -> 6, of which waited for: 6 -> 6; matrix products, arithmetic and copies ran while one was open for 5% -> 6% of each run, Pallas kernels for 0% -> 0%
where the time goes in v1:
time: 599 us; the launch traced here: 598 us
  waiting for transfers between devices  385 us (64%)
  blocking collectives  119 us (20%)
  local copies, waits for them, and re-layouts  32.7 us (5%)
  matrix products  21.3 us (4%)
  other arithmetic  16.3 us (3%)
  between operations  14.1 us (2%)
  starting transfers between devices  8.89 us (1%)
    unnamed x7, waiting for transfers between devices  228 us
    psum x1, blocking collectives, per_device(): total_num, total_den = lax.psum((flat_num, flat_den), 'tp')  64.6 us
    all_to_all x1, waiting for transfers between devices, per_device(): lax.all_to_all(jnp.stack([prompt_values] * lax.axis_size('grp')), 'grp',...  60.4 us
    psum x1, waiting for transfers between devices, per_device(): total_num, total_den = lax.psum((flat_num, flat_den), 'tp')  38.5 us
    all_gather x1, waiting for transfers between devices, per_device(): projected_qkv = lax.all_gather(qkv_share, 'tp', axis=1, tiled=True)  36.5 us
    all_gather x1, blocking collectives, per_device(): lax.all_gather(ffn_in, 'tp', axis=0, tiled=True)  28.2 us
    all_gather x1, blocking collectives, per_device(): lax.all_gather(normed, 'tp', axis=0, tiled=True)  26.6 us
    all_gather x1, waiting for transfers between devices, per_device(): key_piece = lax.all_gather(prompt_keys, 'grp', axis=0, tiled=True)  21.5 us
  transfers between devices with their start and end apart: 6, of which 6 were waited for; matrix products, arithmetic and copies ran while one was open for 6% of the time, Pallas kernels for 0%

profile of v1, /device:TPU:1, one launch (start us, length us, event | category | flops | bytes accessed | tf_op | source)
XLA Modules:
  0.0 597.8 jit_solution(15450793808265596107)
XLA Ops:
  6.5 1.0 fusion.36
  7.6 1.1 slice_reduce_fusion.1
  8.7 0.8 fusion.48
  9.5 26.6 %all-gather = bf16[32,4,3584]{2,1,0:T(4,128)(2,1)S(1)} all-gather(bf16[1,4,3584]{2,1,0:T(4,128)(2,1)S(1)} %fusion.48), channel_id=1, replica_groups=mesh['grp'=8,'tp'=32] {'tp'}, dimensions={0}, use_global_device_ids=true | all-gather | bytes 946176 | tf_op jit(solution)/shard_map/all_gather | solution.py:103
  36.1 1.1 reshape.277
  37.2 2.8 convolution_convert_fusion.1
  40.1 2.5 stack.2
  42.7 8.3 %all-to-all-start = ((bf16[8,128,2048]{2,1,0:T(8,128)(2,1)}), bf16[8,128,2048]{2,1,0:T(8,128)(2,1)}, u32[]{:S(2)}, u32[]{:S(2)}) async-start(bf16[8,128,2048]{2,1,0:T(8,128)(2,1)} %stack.2), calls=%async_computation | async-start | bytes 8388608 | tf_op jit(solution)/shard_map/all_to_all | solution.py:141
  51.0 1.0 copy.73
  52.1 0.2 all-reduce.6.cloned.1.call-start
  52.3 0.1 dynamic_slice.12
  52.5 0.2 select_reduce_fusion.2
  52.6 0.1 select_reduce_fusion.3
  52.8 0.1 iota_compare_fusion.4
  52.8 0.3 multiply_cosine_fusion
  53.2 0.9 compare_and_fusion
  54.0 36.5 %all-gather.5.cloned.1.call-done = bf16[128,8192]{1,0:T(8,128)(2,1)} async-done(((bf16[128,256]{1,0:T(8,128)(2,1)}), bf16[128,8192]{1,0:T(8,128)(2,1)}) %all-gather.5.cloned.1.call-update) | async-done | bytes 2097168 | tf_op jit(solution)/shard_map/all_gather | solution.py:105
  90.5 1.4 slice_convert_fusion
  91.9 0.7 copy.96
  92.6 0.3 subtract_convert_fusion
  92.9 0.1 copy.71
  93.1 1.1 copy-done.3
  94.2 0.2 slice_convert_fusion.2
  94.4 1.3 copy.98
  95.7 1.4 copy.99
  97.1 0.1 copy.72
  97.3 0.5 fusion.74
  97.8 0.1 copy.83
  97.9 1.4 subtract_convert_fusion.1
  99.4 1.1 pad_maximum_fusion
  100.6 0.3 fusion.11
  100.8 60.4 %all-to-all-done = bf16[8,128,2048]{2,1,0:T(8,128)(2,1)} async-done(((bf16[8,128,2048]{2,1,0:T(8,128)(2,1)}), bf16[8,128,2048]{2,1,0:T(8,128)(2,1)}, u32[]{:S(2)}, u32[]{:S(2)}) %all-to-all-start) | async-done | bytes 4194336 | tf_op jit(solution)/shard_map/all_to_all | solution.py:141
  161.2 5.7 copy.97
  166.9 21.5 %all-gather.7.cloned.1.call-done = bf16[1024,2048]{0,1:T(8,128)(2,1)} async-done(((bf16[128,2048]{0,1:T(8,128)(2,1)}), bf16[1024,2048]{0,1:T(8,128)(2,1)}) %all-gather.7.cloned.1.call-update) | async-done | bytes 4194320 | tf_op jit(solution)/shard_map/all_gather | solution.py:139
  188.4 5.1 bitcast_reduce_fusion
  193.5 2.5 fusion
  196.0 1.4 copy.121
  197.3 0.7 fusion.29
  198.0 2.9 copy.80
  200.9 2.9 copy.81
  203.8 0.3 all-reduce.8.cloned.1.call-start
  204.1 3.3 fusion.16
  207.5 1.2 copy.89
  208.7 0.2 copy.82
  209.0 2.8 broadcast_multiply_fusion
  211.7 4.0 mul.269
  215.7 0.1 dynamic-slice_add_fusion
  215.8 1.3 add.147
  217.1 64.6 %psum.15 = f32[128,16]{0,1:T(8,128)S(1)} all-reduce(f32[128,16]{0,1:T(8,128)S(1)} %bitcast.94), channel_id=1, replica_groups=mesh['grp'=8,'tp'=32] {'tp'}, use_global_device_ids=true, to_apply=%region_8.9 | all-reduce | flops 2048 | bytes 16384 | tf_op jit(solution)/shard_map/psum | solution.py:163
  281.7 38.5 %all-reduce.6.cloned.1.call-done = f32[128,4096]{1,0:T(8,128)} async-done(((f32[128,4096]{1,0:T(8,128)}), f32[128,4096]{1,0:T(8,128)}) %all-reduce.6.cloned.1.call-update) | async-done | bytes 2097168 | tf_op jit(solution)/shard_map/psum | solution.py:163
  320.2 1.1 fusion.6
  321.4 1.6 fusion.75
  323.1 0.6 dynamic-slice.6
  324.4 115.3 %all-reduce.8.cloned.1.call-done = f32[128,3584]{1,0:T(8,128)} async-done(((f32[128,3584]{1,0:T(8,128)}), f32[128,3584]{1,0:T(8,128)}) %all-reduce.8.cloned.1.call-update) | async-done | bytes 1835024
  439.7 1.0 multiply_reduce_fusion
  440.7 1.1 fusion.40
  441.9 0.1 fusion.47
  442.0 28.2 %all-gather.1 = bf16[32,4,3584]{2,1,0:T(4,128)(2,1)} all-gather(bf16[1,4,3584]{2,1,0:T(4,128)(2,1)S(1)} %fusion.47), channel_id=1, replica_groups=mesh['grp'=8,'tp'=32] {'tp'}, dimensions={0}, use_global_device_ids=true | all-gather | bytes 946176 | tf_op jit(solution)/shard_map/all_gather | solution.py:195
  470.2 1.7 reshape.284
  471.8 2.7 convolution_bitcast_fusion
  474.5 1.4 convolution_convert_fusion
  476.0 112.7 %all-reduce.10.cloned.1.call-done = bf16[128,3584]{1,0:T(8,128)(2,1)} async-done(((bf16[128,3584]{1,0:T(8,128)(2,1)}), bf16[128,3584]{1,0:T(8,128)(2,1)}) %all-reduce.10.cloned.1.call-update) | async-done | bytes 917520
  588.7 1.0 fusion.34
  589.7 1.5 fusion.43
  (51 shorter events, 0.4 us)
Async XLA Ops:
  6.5 468.0 %copy-start = (bf16[256,3584]{1,0:T(8,128)(2,1)S(1)}, bf16[256,3584]{1,0:T(8,128)(2,1)}, u32[]{:S(2)}) copy-start(bf16[256,3584]{1,0:T(8,128)(2,1)} %param.19) | copy-start | bytes 5505028
  6.5 83.9 %all-gather.5.cloned.1.call-start = ((), (), s32[]{:S(2)}) async-start(), calls=%async_computation.1 | async-start | bytes 2162688 | tf_op jit(solution)/shard_map/all_gather | solution.py:105
  36.1 4.0 copy-start.6
  42.6 8.4 %copy-start.7 = (bf16[128,2048]{1,0:T(8,128)(2,1)S(1)}, bf16[128,2048]{1,0:T(8,128)(2,1)}, u32[]{:S(2)}) copy-start(bf16[128,2048]{1,0:T(8,128)(2,1)} %param.20) | copy-start | bytes 1572868
  42.6 9.7 %copy-start.13 = (s32[128]{0:T(128)S(1)}, s32[128]{0:T(128)}, u32[]{:S(2)}) copy-start(s32[128]{0:T(128)} %param.27) | copy-start | bytes 1540
  42.6 9.8 %copy-start.10 = (s32[80]{0:T(128)S(1)}, s32[80]{0:T(128)}, u32[]{:S(2)}) copy-start(s32[80]{0:T(128)} %param.25) | copy-start | bytes 964
  42.6 9.8 %copy-start.11 = (s32[80]{0:T(128)S(1)}, s32[80]{0:T(128)}, u32[]{:S(2)}) copy-start(s32[80]{0:T(128)} %param.24) | copy-start | bytes 964
  42.6 10.0 %copy-start.12 = (s32[128]{0:T(128)S(1)}, s32[128]{0:T(128)}, u32[]{:S(2)}) copy-start(s32[128]{0:T(128)} %param.26) | copy-start | bytes 1540
  42.7 118.5 %all-to-all-start = ((bf16[8,128,2048]{2,1,0:T(8,128)(2,1)}), bf16[8,128,2048]{2,1,0:T(8,128)(2,1)}, u32[]{:S(2)}, u32[]{:S(2)}) async-start(bf16[8,128,2048]{2,1,0:T(8,128)(2,1)} %stack.2), calls=%async_computation | async-start | bytes 8388608 | tf_op jit(solution)/shard_map/all_to_all | solution.py:141
  51.0 137.4 %all-gather.7.cloned.1.call-start = ((), (), s32[]{:S(2)}) async-start(), calls=%async_computation.2 | async-start | bytes 4718592 | tf_op jit(solution)/shard_map/all_gather | solution.py:139
  52.1 268.2 %all-reduce.6.cloned.1.call-start = ((), (), s32[]{:S(2)}) async-start(), calls=%async_computation.3 | async-start | bytes 4194304 | tf_op jit(solution)/shard_map/psum | solution.py:163
  92.6 1.6 copy-start.3
  95.7 1.6 copy-start.14
  97.9 2.6 copy-start.4
  188.4 5.1 copy-start.2
  188.4 5.1 copy-start.9
  203.8 5.1 copy-start.1
  203.8 235.8 %all-reduce.8.cloned.1.call-start = ((), (), s32[]{:S(2)}) async-start(), calls=%async_computation.4 | async-start | bytes 3670016
  211.7 109.7 %copy-start.5 = (bf16[128,3584]{1,0:T(8,128)(2,1)S(1)}, bf16[128,3584]{1,0:T(8,128)(2,1)}, u32[]{:S(2)}) copy-start(bf16[128,3584]{1,0:T(8,128)(2,1)} %param.17) | copy-start | bytes 2752516
  321.4 1.7 copy-start.15
  321.4 119.3 %copy-start.8 = (bf16[4,3584]{1,0:T(4,128)(2,1)S(1)}, bf16[4,3584]{1,0:T(4,128)(2,1)}, u32[]{:S(2)}) copy-start(bf16[4,3584]{1,0:T(4,128)(2,1)} %param.14) | copy-start | bytes 86020
  323.1 265.7 %all-reduce.10.cloned.1.call-start = ((), (), s32[]{:S(2)}) async-start(), calls=%async_computation.5 | async-start | bytes 1835008
Sparse Core Ops, SparseCore 0:
  40.2 50.2 all-gather.4
  92.2 96.1 all-gather.6
  204.0 116.2 all-reduce.5
  323.4 116.2 all-reduce.7
  476.1 112.5 all-reduce.9
